TPU v7x, 32 devices: a whole 2x2x4 slice. The times are simulated.
32 devices in a mesh: zone: 8 (over z, y), band: 4 (over x, core).
Axes of the slice: x: 2, y: 2, z: 4, core: 2. Of those that a mesh axis runs over, the one named last changes fastest.
Arguments:
- pixels: float32 [4096, 32, 128], P(('zone', 'band')), may hold values from -6 to 6
- inv_var: float32 [4096, 32, 128], P(('zone', 'band')), may hold values from 0.25 to 4
- tile_offset: float32 [2, 4096], P(None, ('zone', 'band')), may hold values from 12 to 116, as said below
- psf_amp: float32 [3, 4096], P(None, ('zone', 'band')), may hold values from 0.3 to 1
- psf_sigma: float32 [3, 4096], P(None, ('zone', 'band')), may hold values from 0.9 to 2
- tile_blob: int32 [4096], P(('zone', 'band')), may hold values from 0 to 511, as said below
- tile_band: int32 [4096], P(('zone', 'band')), may hold values from 0 to 2
- source_pos: float32 [2, 4096], P(None, 'zone'), may hold values from -5.3 to 5.3
- edge_rows: int32 [1024], P('zone'), may hold values from 0 to 511, as said below
- blob_members: int32 [512, 16], P('zone'), may hold values from 0 to 639, as said below
- sources_per_blob: int32 [512], P('zone'), may hold values from 1 to 16, as said below
Outputs:
- fluxes: float32 [3, 4096], P(None, 'zone')
Inputs may be any that keep to these rules, and one draw needn't show every extreme that they name: `tile_blob`: blob b lies in zone b // 64. Of one device's 128 tiles at most 32 cover blobs of one zone, and in every draw some zone receives exactly 32 tiles from every device of each band group. `edge_rows`: per zone, 64 lower edge rows then 64 upper edge rows, local row numbers, all 128 distinct. `blob_members`: slots at or beyond the blob's count hold 0. Every source is the live member of exactly one blob: a zone's lower edge rows belong to blobs of the previous zone and its upper edge rows to blobs of the next zone, except the first zone's lower and the last zone's upper rows, which stay in their own zone; the first zone never names the first 64 entries, the last zone never the last 64. `sources_per_blob`: the counts of one zone sum to 512; in every zone some blob has 16. `tile_offset`: row offsets lie within 12 to 20.
All inputs are finite; a program needn't handle non-finite values.
Results may differ from a plain program's by a relative error of at most 0.0003.
Values sent between devices are 32-bit elements; how exact they have to be, the bound alone decides.
A program may use at most 64 MiB of HBM per device.

v0:
```python
import functools

import jax
import jax.numpy as jnp
from jax import lax
from jax.experimental import pallas as pl
from jax.experimental.pallas import tpu as pltpu
from jax.sharding import PartitionSpec as P

FILTER_BANDS = 3
COMPS = 3
MAX_SOURCES = 16
LANES = 128
PACK = LANES // MAX_SOURCES
ROWS = 24
TILES_STEP = 16
CHUNK = 32
PRIOR = 1.0

VMEM = pl.BlockSpec(memory_space=pltpu.VMEM)
SMEM = pl.BlockSpec(memory_space=pltpu.SMEM)


def exchange(block, moves, pick, slot, slots, sizes, ident, label_row=None):
    zones, bands = sizes
    piece = block.shape[-2:] if pick is None else block.shape[1:]

    def kernel(x_ref, o_ref, *refs):
        send_sem, recv_sem, own_sem = refs[-3:]
        zone = lax.axis_index("zone")
        band = lax.axis_index("band")
        targets = [
            (lax.rem(zone + dz + zones, zones), lax.rem(band + db + bands, bands))
            for dz, db in moves
        ]
        barrier = pltpu.get_barrier_semaphore()
        for target in targets:
            pl.semaphore_signal(
                barrier, inc=1, device_id=target, device_id_type=pl.DeviceIdType.MESH
            )
        own_src = x_ref if pick is None else x_ref.at[pick(zone, band)]
        own = pltpu.make_async_copy(own_src, o_ref.at[slot(0, 0, zone, band)], own_sem)
        own.start()
        pl.semaphore_wait(barrier, len(moves))
        copies = []
        for order, ((dz, db), target) in enumerate(zip(moves, targets)):
            copy = pltpu.make_async_remote_copy(
                src_ref=x_ref if pick is None else x_ref.at[pick(*target)],
                dst_ref=o_ref.at[slot(dz, db, zone, band)],
                send_sem=send_sem.at[order],
                recv_sem=recv_sem.at[order],
                device_id=target,
                device_id_type=pl.DeviceIdType.MESH,
            )
            copy.start()
            copies.append(copy)
        own.wait()
        for copy in copies:
            copy.wait()
        if label_row is not None:
            code_ref = refs[0]
            groups = piece[0] // ROWS
            for order in range(slots * groups):
                at = order % groups * ROWS + label_row
                code_ref[order : order + 1, :] = o_ref[order // groups, at : at + 1, :].astype(
                    jnp.int32
                )

    out_shape = [jax.ShapeDtypeStruct((slots,) + piece, block.dtype)]
    if label_row is not None:
        out_shape.append(jax.ShapeDtypeStruct((slots * piece[0] // ROWS, LANES), jnp.int32))
    return pl.pallas_call(
        kernel,
        out_shape=out_shape,
        in_specs=[VMEM],
        out_specs=[VMEM] * len(out_shape),
        scratch_shapes=[
            pltpu.SemaphoreType.DMA((len(moves),)),
            pltpu.SemaphoreType.DMA((len(moves),)),
            pltpu.SemaphoreType.DMA,
        ],
        compiler_params=pltpu.CompilerParams(collective_id=ident, has_side_effects=True),
    )(block)


def lane_take(row, index):
    table = jnp.broadcast_to(row, index.shape)
    return jnp.take_along_axis(table, index, axis=1, mode="promise_in_bounds")


def lookup(rows, index):
    found = jnp.zeros(index.shape, rows[0].dtype)
    low = index & (LANES - 1)
    for part, row in enumerate(rows):
        found = jnp.where(index // LANES == part, lane_take(row, low), found)
    return found


class Catalog:
    def __init__(self, sources, edge, blobs):
        self.parts = sources // LANES
        self.edge_row = 2 * self.parts
        self.count_row = self.edge_row + 1
        self.member_row = -(-(self.count_row + 1) // 8) * 8
        self.member_rows = blobs // PACK
        self.rows = self.member_row + -(-self.member_rows // 8) * 8
        self.sources, self.edge, self.blobs = sources, edge, blobs

    def pack(self, source_ref, edge_ref, member_ref, count_ref, sigma_ref, out_ref, spread_ref):
        out_ref[...] = jnp.zeros_like(out_ref)
        for coord in range(2):
            for part in range(self.parts):
                at = coord * self.parts + part
                out_ref[at : at + 1, :] = source_ref[
                    coord : coord + 1, part * LANES : (part + 1) * LANES
                ]
        out_ref[self.edge_row : self.edge_row + 1, :] = edge_ref[...].astype(jnp.float32)
        out_ref[self.count_row : self.count_row + 1, : self.blobs] = count_ref[...].astype(
            jnp.float32
        )
        seats = [
            member_ref[pl.ds(seat, self.member_rows, stride=PACK), :].astype(jnp.float32)
            for seat in range(PACK)
        ]
        out_ref[self.member_row : self.member_row + self.member_rows, :] = jnp.concatenate(
            seats, axis=1
        )
        sigma = sigma_ref[...]
        spread_ref[...] = 0.5 / (sigma * sigma)

    def members(self, ref, zone):
        return ref[zone, self.member_row : self.member_row + self.member_rows, :].astype(jnp.int32)

    def edges(self, ref, zone):
        return ref[zone, self.edge_row : self.edge_row + 1, :].astype(jnp.int32)

    def live(self, ref, zone):
        shape = (self.member_rows, LANES)
        lane = lax.broadcasted_iota(jnp.int32, shape, 1)
        row = lax.broadcasted_iota(jnp.int32, shape, 0)
        counts = ref[zone, self.count_row : self.count_row + 1, :].astype(jnp.int32)
        held = lane_take(counts, row * PACK + lane // MAX_SOURCES)
        return (lane % MAX_SOURCES) < held


def resolve(cat, zones, cat_ref, edge_ref, table_ref):
    def edge_body(zone, carry):
        index = jnp.broadcast_to(cat.edges(cat_ref, zone), (8, LANES))
        for coord in range(2):
            rows = [
                cat_ref[zone, coord * cat.parts + part : coord * cat.parts + part + 1, :]
                for part in range(cat.parts)
            ]
            edge_ref[coord, zone] = lookup(rows, index)
        return carry

    lax.fori_loop(0, zones, edge_body, 0)

    def member_body(zone, carry):
        member = cat.members(cat_ref, zone)
        before = jnp.maximum(zone - 1, 0)
        after = jnp.minimum(zone + 1, zones - 1)
        lane = lax.broadcasted_iota(jnp.int32, (8, LANES), 1)
        low = member < cat.edge
        high = member >= cat.edge + cat.sources
        own = jnp.clip(member - cat.edge, 0, cat.sources - 1)
        rim = jnp.where(low, cat.edge + member, jnp.where(high, member - cat.edge - cat.sources, 0))
        start = pl.multiple_of(zone * cat.member_rows, 8)
        for coord in range(2):
            rows = [
                cat_ref[zone, coord * cat.parts + part : coord * cat.parts + part + 1, :]
                for part in range(cat.parts)
            ]
            table = jnp.where(lane >= cat.edge, edge_ref[coord, before], edge_ref[coord, after])
            at_rim = lane_take(table[:1], rim)
            table_ref[coord, pl.ds(start, cat.member_rows), :] = jnp.where(
                low | high, at_rim, lookup(rows, own)
            )
        table_ref[2, pl.ds(start, cat.member_rows), :] = cat.live(cat_ref, zone).astype(jnp.float32)
        return carry

    lax.fori_loop(0, zones, member_body, 0)


def tile_kernel(
    cat, zones, groups,
    blob_ref, band_ref, shift_ref, amp_ref, spread_ref,
    cat_ref, pixel_ref, weight_ref,
    out_ref, edge_ref, table_ref, line_ref, used_ref,
):
    step = pl.program_id(0)
    height = pixel_ref.shape[1]

    @pl.when(step == 0)
    def _():
        out_ref[...] = jnp.zeros_like(out_ref)
        for zone in range(zones):
            used_ref[zone] = 0
        resolve(cat, zones, cat_ref, edge_ref, table_ref)

    half = MAX_SOURCES // 2
    shape = (MAX_SOURCES, LANES)
    lane = lax.broadcasted_iota(jnp.int32, shape, 1)
    sub = lax.broadcasted_iota(jnp.int32, shape, 0)
    lane_f = lane.astype(jnp.float32)
    keep = (lane % half) == (sub % half)
    tall = (height, LANES)
    tall_lane = lax.broadcasted_iota(jnp.int32, tall, 1)
    row_f = lax.broadcasted_iota(jnp.int32, tall, 0).astype(jnp.float32)
    eight_lane = tall_lane[:8]
    comp = (eight_lane[:1] // half) % COMPS
    width = COMPS * half
    high_part = (tall_lane < width) | (tall_lane >= 2 * width)
    used_part = tall_lane < 3 * width
    blank = jnp.zeros((LANES - 3 * width, LANES), jnp.float32)

    for slot in range(pixel_ref.shape[0]):
        tile = step * pixel_ref.shape[0] + slot
        blob = blob_ref[tile]
        at = blob // PACK
        offset = (blob % PACK) * MAX_SOURCES
        table = [
            jnp.broadcast_to(table_ref[k, pl.ds(at, 1), :], shape) for k in range(3)
        ]
        col_pos = jnp.sum(
            jnp.where(lane == offset + sub, table[1], 0.0), axis=1, keepdims=True
        )
        spread = [spread_ref[g, tile] for g in range(COMPS)]
        amp = [amp_ref[g, tile] for g in range(COMPS)]
        row_spread = jnp.where(comp == 0, spread[0], jnp.where(comp == 1, spread[1], spread[2]))
        row_amp = jnp.where(comp == 0, amp[0], jnp.where(comp == 1, amp[1], amp[2]))
        dcol = lane_f - shift_ref[1, tile] - col_pos
        dcol = dcol * dcol
        cols = [jnp.exp(-spread[g] * dcol) for g in range(COMPS)]
        cols_head = [col.astype(jnp.bfloat16).astype(jnp.float32) for col in cols]
        cols_tail = [col - head for col, head in zip(cols, cols_head)]
        root = jnp.sqrt(weight_ref[slot])
        image = root * pixel_ref[slot]
        image_head = image.astype(jnp.bfloat16).astype(jnp.float32)
        line_ref[slot, 0] = root
        line_ref[slot, 1] = image_head
        line_ref[slot, 2] = image - image_head
        rights = []
        for h in range(2):
            index = offset + h * half + eight_lane % half
            row_pos = jnp.take_along_axis(table[0][:8], index, axis=1, mode="promise_in_bounds")
            live = jnp.take_along_axis(table[2][:8], index, axis=1, mode="promise_in_bounds")
            drow = row_f - shift_ref[0, tile] - row_pos[:1]
            rows = jnp.exp(-row_spread * (drow * drow)) * (row_amp * live[:1])
            rows_head = rows.astype(jnp.bfloat16).astype(jnp.float32)
            line_ref[slot, 3 + h] = jnp.where(
                used_part, jnp.where(high_part, rows_head, rows - rows_head), 0.0
            )
            span = slice(h * half, (h + 1) * half)
            heads = [c[span] for c in cols_head]
            rights.append(
                jnp.concatenate(
                    heads + heads + [c[span] for c in cols_tail] + [blank], axis=0
                ).astype(jnp.bfloat16)
            )

        def render(chunk):
            models = []
            for h in range(2):
                left = []
                for i in range(chunk * CHUNK, (chunk + 1) * CHUNK, 2):
                    pair = jnp.concatenate(
                        [
                            jnp.broadcast_to(
                                line_ref[slot, 3 + h, i + d : i + d + 1, :], (half, LANES)
                            )
                            for d in range(2)
                        ],
                        axis=0,
                    )
                    left.append(jnp.where(keep, pair, 0.0).astype(jnp.bfloat16))
                models.append(
                    lax.dot_general(
                        jnp.concatenate(left, axis=0), rights[h], (((1,), (0,)), ((), ())),
                        preferred_element_type=jnp.float32,
                    )
                )
            return models

        product = None
        chunks = height // CHUNK
        ahead = render(0)
        for chunk in range(chunks):
            models = ahead
            if chunk + 1 < chunks:
                ahead = render(chunk + 1)
            heads, tails, lines = [], [], []
            for at_row in range(CHUNK):
                i = chunk * CHUNK + at_row
                span = slice(at_row * half, (at_row + 1) * half)
                weight = jnp.broadcast_to(line_ref[slot, 0, i : i + 1, :], shape)
                scaled = jnp.concatenate([models[0][span], models[1][span]], axis=0) * weight
                head = scaled.astype(jnp.bfloat16)
                heads.append(head)
                tails.append((scaled - head.astype(jnp.float32)).astype(jnp.bfloat16))
                lines.append(
                    jnp.concatenate(
                        [
                            jnp.broadcast_to(line_ref[slot, k, i : i + 1, :], (half, LANES))
                            for k in (1, 2)
                        ],
                        axis=0,
                    ).astype(jnp.bfloat16)
                )
            factor = jnp.concatenate(
                [jnp.concatenate(heads, axis=1), jnp.concatenate(tails, axis=1)], axis=0
            )
            left = jnp.concatenate([factor, jnp.concatenate(lines, axis=1)], axis=0)
            part = lax.dot_general(
                left, factor, (((1,), (1,)), ((), ())), preferred_element_type=jnp.float32
            )
            product = part if product is None else product + part
        folded = product[:, :16] + product[:, 16:]
        normal = folded[:16] + folded[16:32]
        vector = folded[32:40] + folded[40:48]
        zone = blob // cat.blobs
        code = band_ref[tile] * cat.blobs + blob % cat.blobs
        eight = lax.broadcasted_iota(jnp.int32, vector.shape, 0)
        tailrows = jnp.where(
            eight == 0, vector, jnp.where(eight == 1, code.astype(jnp.float32), 0.0)
        )
        entry = jnp.concatenate([normal, tailrows], axis=0)
        entry = jnp.concatenate(
            [entry, jnp.zeros((ROWS, LANES - MAX_SOURCES), jnp.float32)], axis=1
        )
        order = used_ref[zone]
        used_ref[zone] = order + 1
        seat = order % PACK
        entry = pltpu.roll(entry, seat * MAX_SOURCES, 1)
        place = zone * groups + order // PACK
        out_ref[place] = out_ref[place] + entry


def tile_terms(cat, zones, groups, blob, band, shift, amp, spread, catalogs, pixels, weights):
    tiles, height, width = pixels.shape
    per = TILES_STEP
    while tiles % per:
        per -= 1
    block = pl.BlockSpec((per, height, width), lambda s: (s, 0, 0))
    return pl.pallas_call(
        functools.partial(tile_kernel, cat, zones, groups),
        grid=(tiles // per,),
        out_shape=jax.ShapeDtypeStruct((zones * groups, ROWS, LANES), jnp.float32),
        in_specs=[SMEM] * 5 + [VMEM, block, block],
        out_specs=pl.BlockSpec((zones * groups, ROWS, LANES), lambda s: (0, 0, 0)),
        scratch_shapes=[
            pltpu.VMEM((2, zones, 8, LANES), jnp.float32),
            pltpu.VMEM((3, zones * cat.member_rows, LANES), jnp.float32),
            pltpu.VMEM((per, 5, height, width), jnp.float32),
            pltpu.SMEM((zones,), jnp.int32),
        ],
        compiler_params=pltpu.CompilerParams(dimension_semantics=("arbitrary",)),
    )(blob, band, shift, amp, spread, catalogs, pixels, weights)


def gather_kernel(capacity, groups, code_ref, got_ref, total_ref):
    total_ref[...] = jnp.zeros_like(total_ref)
    lane = lax.broadcasted_iota(jnp.int32, (ROWS, LANES), 1) // MAX_SOURCES

    def body(group, carry):
        block = got_ref[group]
        for seat in range(min(PACK, capacity)):
            code = code_ref[group, seat * MAX_SOURCES]
            to = code % PACK
            moved = pltpu.roll(block, ((to - seat + PACK) % PACK) * MAX_SOURCES, 1)
            place = code // PACK
            total_ref[place] = total_ref[place] + jnp.where(lane == to, moved, 0.0)
        return carry

    lax.fori_loop(0, got_ref.shape[0], body, 0)


def solve_group(block):
    row = lax.broadcasted_iota(jnp.int32, (ROWS, LANES), 0)
    lane = lax.broadcasted_iota(jnp.int32, (ROWS, LANES), 1)
    column = lane % MAX_SOURCES
    first = lane - column
    block = block + jnp.where(row == column, PRIOR, 0.0)
    scale = jnp.ones((1, LANES), jnp.float32)
    for k in range(MAX_SOURCES):
        taken = jnp.take_along_axis(block, first + k, axis=1, mode="promise_in_bounds")
        pivot = taken[k : k + 1]
        across = block[k : k + 1]
        scale = jnp.where(column[:1] == k, across, scale)
        ratio = jnp.where(column[:1] == k, 0.0, across / pivot)
        block = block - taken * ratio
    return block[MAX_SOURCES : MAX_SOURCES + 1] / scale


def finish_kernel(
    cat, zones, bands, share, total_ref, cat_ref, out_ref,
    got_ref, solved_ref, flux_ref, pick_ref,
    send_sum, recv_sum, own_sum, send_flux, recv_flux, own_flux,
):
    zone = lax.axis_index("zone")
    band = lax.axis_index("band")
    moves = [(dz, db) for dz in (0, 1, -1) for db in range(bands) if dz or db]
    targets = [
        (lax.rem(zone + dz + zones, zones), lax.rem(band + db, bands)) for dz, db in moves
    ]
    barrier = pltpu.get_barrier_semaphore()
    for target in targets:
        pl.semaphore_signal(barrier, inc=1, device_id=target, device_id_type=pl.DeviceIdType.MESH)
    own = pltpu.make_async_copy(total_ref.at[band], got_ref.at[band], own_sum)
    own.start()
    pl.semaphore_wait(barrier, len(moves))
    sums = []
    for order in range(bands - 1):
        target = targets[order]
        copy = pltpu.make_async_remote_copy(
            src_ref=total_ref.at[target[1]],
            dst_ref=got_ref.at[band],
            send_sem=send_sum.at[order],
            recv_sem=recv_sum.at[order],
            device_id=target,
            device_id_type=pl.DeviceIdType.MESH,
        )
        copy.start()
        sums.append(copy)

    edges = cat.edges(cat_ref, zone)
    rows = cat.member_rows
    source = lax.broadcasted_iota(jnp.int32, (cat.sources, LANES), 0)
    for side in range(3):
        near = lax.rem(zone + side - 1 + zones, zones)
        member = cat.members(cat_ref, near)
        live = cat.live(cat_ref, near)
        if side == 0:
            valid = (member >= cat.edge + cat.sources) & (zone > 0)
            target = lane_take(edges, jnp.where(valid, member - cat.edge - cat.sources, 0))
        elif side == 1:
            valid = (member >= cat.edge) & (member < cat.edge + cat.sources)
            target = member - cat.edge
        else:
            valid = (member < cat.edge) & (zone < zones - 1)
            target = lane_take(edges, jnp.where(valid, member + cat.edge, 0))
        target = jnp.where(valid & live, target, -1)
        for row in range(rows):
            hit = source == target[row : row + 1, :]
            pick_ref[side, :, row * LANES : (row + 1) * LANES] = jnp.where(hit, 1.0, 0.0).astype(
                jnp.bfloat16
            )

    own.wait()
    for copy in sums:
        copy.wait()
    for group in range(share):
        span = slice(group * ROWS, (group + 1) * ROWS)
        block = got_ref[0, span, :]
        for other in range(1, bands):
            block = block + got_ref[other, span, :]
        solved_ref[group : group + 1, :] = solve_group(block)
    if solved_ref.shape[0] > share:
        solved_ref[share:, :] = jnp.zeros((solved_ref.shape[0] - share, LANES), jnp.float32)

    own = pltpu.make_async_copy(solved_ref, flux_ref.at[bands + band], own_flux)
    own.start()
    copies = []
    for order, ((dz, db), target) in enumerate(zip(moves, targets)):
        copy = pltpu.make_async_remote_copy(
            src_ref=solved_ref,
            dst_ref=flux_ref.at[(1 - dz) * bands + band],
            send_sem=send_flux.at[order],
            recv_sem=recv_flux.at[order],
            device_id=target,
            device_id_type=pl.DeviceIdType.MESH,
        )
        copy.start()
        copies.append(copy)
    own.wait()
    for copy in copies:
        copy.wait()

    total = jnp.zeros((16, cat.sources), jnp.float32)
    for side in range(3):
        parts = []
        for band_row in range(FILTER_BANDS):
            lines = []
            for row in range(rows):
                group = band_row * rows + row
                at = group % share
                lines.append(flux_ref[side * bands + group // share, at : at + 1, :])
            parts.append(jnp.concatenate(lines, axis=1))
        values = jnp.concatenate(parts, axis=0)
        pieces = []
        for _ in range(3):
            piece = values.astype(jnp.bfloat16).astype(jnp.float32)
            values = values - piece
            pieces.append(piece)
        pieces.append(jnp.zeros((16 - 3 * FILTER_BANDS, values.shape[1]), jnp.float32))
        left = jnp.concatenate(pieces, axis=0).astype(jnp.bfloat16)
        total = total + lax.dot_general(
            left, pick_ref[side], (((1,), (1,)), ((), ())), preferred_element_type=jnp.float32
        )
    out_ref[...] = total[0:3] + total[3:6] + total[6:9]


def on_device(
    sizes, pixels, inv_var, tile_offset, psf_amp, psf_sigma, tile_blob, tile_band,
    source_pos, edge_rows, blob_members, sources_per_blob,
):
    zones, bands = sizes
    blobs = sources_per_blob.shape[0]
    sources = source_pos.shape[1]
    tiles = pixels.shape[0]
    cat = Catalog(sources, edge_rows.shape[0] // 2, blobs)
    capacity = max(2, (2 * tiles + zones - 1) // zones)
    groups = -(-capacity // PACK)
    systems = FILTER_BANDS * blobs // PACK
    share = systems // bands
    zone_moves = [(d, 0) for d in range(1, zones)]

    packed, spread = pl.pallas_call(
        cat.pack,
        out_shape=(
            jax.ShapeDtypeStruct((cat.rows, LANES), jnp.float32),
            jax.ShapeDtypeStruct(psf_sigma.shape, jnp.float32),
        ),
        in_specs=[VMEM] * 5,
        out_specs=(VMEM, VMEM),
    )(
        source_pos, edge_rows.reshape(1, -1), blob_members, sources_per_blob.reshape(1, -1),
        psf_sigma,
    )
    (catalogs,) = exchange(packed, zone_moves, None, lambda dz, db, z, b: z, zones, sizes, 0)
    terms = tile_terms(
        cat, zones, groups, tile_blob, tile_band, tile_offset, psf_amp, spread, catalogs,
        pixels, inv_var,
    )
    got, codes = exchange(
        terms.reshape(zones, groups * ROWS, LANES),
        zone_moves, lambda z, b: z, lambda dz, db, z, b: z, zones, sizes, 1,
        MAX_SOURCES + 1,
    )
    got = got.reshape(zones * groups, ROWS, LANES)
    totals = pl.pallas_call(
        functools.partial(gather_kernel, capacity, groups),
        out_shape=jax.ShapeDtypeStruct((systems, ROWS, LANES), jnp.float32),
        in_specs=[SMEM, VMEM],
        out_specs=VMEM,
    )(codes, got)
    near = 3 * bands - 1
    seats = -(-share // 8) * 8
    return pl.pallas_call(
        functools.partial(finish_kernel, cat, zones, bands, share),
        out_shape=jax.ShapeDtypeStruct((FILTER_BANDS, sources), jnp.float32),
        in_specs=[VMEM, VMEM],
        out_specs=VMEM,
        scratch_shapes=[
            pltpu.VMEM((bands, share * ROWS, LANES), jnp.float32),
            pltpu.VMEM((seats, LANES), jnp.float32),
            pltpu.VMEM((3 * bands, seats, LANES), jnp.float32),
            pltpu.VMEM((3, sources, cat.member_rows * LANES), jnp.bfloat16),
            pltpu.SemaphoreType.DMA((bands - 1,)),
            pltpu.SemaphoreType.DMA((bands - 1,)),
            pltpu.SemaphoreType.DMA,
            pltpu.SemaphoreType.DMA((near,)),
            pltpu.SemaphoreType.DMA((near,)),
            pltpu.SemaphoreType.DMA,
        ],
        compiler_params=pltpu.CompilerParams(collective_id=2, has_side_effects=True),
    )(totals.reshape(bands, share * ROWS, LANES), catalogs)


def solution(mesh):
    sizes = (mesh.shape["zone"], mesh.shape["band"])
    return jax.shard_map(
        functools.partial(on_device, sizes),
        mesh=mesh,
        in_specs=(
            P(("zone", "band"), None, None),
            P(("zone", "band"), None, None),
            P(None, ("zone", "band")),
            P(None, ("zone", "band")),
            P(None, ("zone", "band")),
            P(("zone", "band")),
            P(("zone", "band")),
            P(None, "zone"),
            P("zone"),
            P("zone", None),
            P("zone"),
        ),
        out_specs=P(None, "zone"),
        check_vma=False,
    )
```

profile of v0, /device:TPU:0, one launch (start us, length us, event | category | flops | bytes accessed | tf_op | source)
XLA Modules:
  0.0 83.0 jit_solution(13189925229444331367)
XLA Ops:
  0.0 1.4 %copy.12.member_ref = s32[64,16]{1,0:T(8,128)} copy(s32[64,16]{0,1:T(8,128)} %param.20) | data formatting | bytes 8192 | tf_op args[9]
  1.4 1.5 %shard_map.109 = (f32[24,128]{1,0:T(8,128)}, f32[3,128]{1,0:T(4,128)}) custom-call(f32[2,512]{1,0:T(2,128)} %source_ref.1, s32[1,128]{1,0:T(1,128)} %bitcast.8, s32[64,16]{1,0:T(8,128)} %copy.12.member_ref, s32[1,64]{1,0:T(1,128)} %bitcast.9, f32[3,128]{1,0:T(4,128)} %sigma_ref.1), custom_call_target="tpu_custom_call" | custom-call | tf_op jit(solution)/shard_map/pallas_call | solution.py:518
  2.9 10.3 %shard_map.110.cat_ref = f32[8,24,128]{2,1,0:T(8,128)} custom-call(f32[24,128]{1,0:T(8,128)} %get-tuple-element.10.x_ref), custom_call_target="tpu_custom_call" | custom-call | tf_op jit(solution)/shard_map/pallas_call | solution.py:72
  13.2 32.7 %shard_map.111 = f32[32,24,128]{2,1,0:T(8,128)} custom-call(s32[128]{0:T(128)} %blob_ref.1, s32[128]{0:T(128)} %band_ref.1, f32[2,128]{1,0:T(2,128)} %shift_ref.1, f32[3,128]{1,0:T(4,128)} %amp_ref.1, f32[3,128]{1,0:T(4,128)} %get-tuple-element.9.spread_ref, f32[8,24,128]{2,1,0:T(8,128)} %shard_map.110.cat_ref, f32[128,32,128]{2,1,0:T(8,128)} %pixel_ref.1, ...), custom_call_target="tpu_custom_call" | custom-call | tf_op jit(solution)/shard_map/pallas_call | solution.py:345
  45.8 11.6 %shard_map.112 = (f32[8,96,128]{2,1,0:T(8,128)}, s32[32,128]{1,0:T(8,128)}) custom-call(f32[8,96,128]{2,1,0:T(8,128)} %bitcast.5), custom_call_target="tpu_custom_call" | custom-call | tf_op jit(solution)/shard_map/pallas_call | solution.py:72
  57.4 5.8 %shard_map.113 = f32[24,24,128]{2,1,0:T(8,128)} custom-call(s32[32,128]{1,0:T(8,128)} %get-tuple-element.11.code_ref, f32[32,24,128]{2,1,0:T(8,128)} %bitcast.7), custom_call_target="tpu_custom_call" | custom-call | tf_op jit(solution)/shard_map/pallas_call | solution.py:541
  63.2 18.4 %shard_map.114 = f32[3,512]{1,0:T(4,128)} custom-call(f32[4,144,128]{2,1,0:T(8,128)} %bitcast.6, f32[8,24,128]{2,1,0:T(8,128)} %shard_map.110.cat_ref), custom_call_target="tpu_custom_call" | custom-call | tf_op jit(solution)/shard_map/pallas_call | solution.py:549
  81.7 1.3 %copy.14 = f32[3,512]{1,0:T(4,128)} copy(f32[3,512]{1,0:T(4,128)} %shard_map.114) | data formatting | bytes 12288
where the time goes:
time: 83.4 us; the launch traced here: 83 us
  Pallas kernels  80.2 us (96%)
  local copies, waits for them, and re-layouts  2.68 us (3%)
    pallas_call x1, Pallas kernels, tile_terms(): pl.pallas_call(functools.partial(tile_kernel, cat, zones, groups), grid=(...  32.7 us
    pallas_call x2, Pallas kernels, exchange(): pl.pallas_call(kernel, out_shape=out_shape, in_specs=[VMEM], out_specs=[V...  21.8 us
    pallas_call x1, Pallas kernels, on_device(): pl.pallas_call(functools.partial(finish_kernel, cat, zones, bands, share)...  18.4 us
    pallas_call x1, Pallas kernels, on_device(): pl.pallas_call(functools.partial(gather_kernel, capacity, groups), out_sh...  5.82 us
    unnamed x2, local copies, waits for them, and re-layouts  2.68 us

commit v1 on v0

v1 whole, which is shorter than its diff:
```python
import functools
import math

import jax
import jax.numpy as jnp
from jax import lax
from jax.experimental import pallas as pl
from jax.experimental.pallas import tpu as pltpu
from jax.sharding import PartitionSpec as P

FILTER_BANDS = 3
COMPS = 3
SLOTS = 16
HALF = SLOTS // 2
LANES = 128
SEATS = 4
SEAT = LANES // SEATS
TILES_STEP = 16
PRIOR = 1.0
FAR = 1.0e4
LOG2E = math.log2(math.e)

VMEM = pl.BlockSpec(memory_space=pltpu.VMEM)
SMEM = pl.BlockSpec(memory_space=pltpu.SMEM)
ANY = pl.BlockSpec(memory_space=pl.ANY)
MESH = pl.DeviceIdType.MESH


def iota(shape, axis):
    return lax.broadcasted_iota(jnp.int32, shape, axis)


def take(table, index):
    return jnp.take_along_axis(table, index, axis=1, mode="promise_in_bounds")


def spread_rows(row, shape):
    return jnp.broadcast_to(row, shape)


def lookup(rows, index):
    found = jnp.zeros(index.shape, rows[0].dtype)
    low = index & (LANES - 1)
    for part, row in enumerate(rows):
        hit = take(spread_rows(row, index.shape), low)
        found = jnp.where(index // LANES == part, hit, found)
    return found


class Sizes:
    def __init__(self, zones, bands, sources, edge, blobs, tiles):
        self.zones, self.bands = zones, bands
        self.sources, self.edge, self.blobs, self.tiles = sources, edge, blobs, tiles
        self.parts = sources // LANES
        self.member_row = -(-2 * self.parts // 8) * 8
        self.edge_row = self.member_row + HALF
        self.cat_rows = self.edge_row + 8
        self.sent_rows = self.edge_row + 2
        capacity = max(SEATS, (2 * tiles + zones - 1) // zones)
        self.capacity = -(-capacity // SEATS) * SEATS
        self.rest = self.capacity // SEATS
        self.rows = -(-(self.capacity + self.rest) // 8) * 8
        self.share = blobs // bands
        self.systems = FILTER_BANDS * self.share
        self.block = -(-self.systems // 8) * 8
        self.third = self.block // FILTER_BANDS
        self.entries = zones * self.capacity


def catalog_kernel(
    sz, source_ref, edge_ref, member_ref, count_ref, out_ref, pack_ref, send_sem, recv_sem, own_sem
):
    zones = sz.zones
    zone = lax.axis_index("zone")
    band = lax.axis_index("band")
    barrier = pltpu.get_barrier_semaphore()
    targets = [(lax.rem(zone + dz, zones), band) for dz in range(1, zones)]
    for target in targets:
        pl.semaphore_signal(barrier, inc=1, device_id=target, device_id_type=MESH)
    shape = (8, LANES)
    edges = spread_rows(edge_ref[...], shape)
    for coord in range(2):
        rows = []
        for part in range(sz.parts):
            row = source_ref[coord : coord + 1, part * LANES : (part + 1) * LANES]
            pack_ref[coord * sz.parts + part : coord * sz.parts + part + 1, :] = row
            rows.append(row)
        at = sz.edge_row + coord
        pack_ref[at : at + 1, :] = lookup(rows, edges)[:1]
    slot = iota((SLOTS, sz.blobs), 0)
    member = jnp.where(slot < count_ref[...], member_ref[...], -1).astype(jnp.float32)
    pack_ref[sz.member_row : sz.member_row + HALF, :] = jnp.concatenate(
        [member[:HALF], member[HALF:]], axis=1
    )
    sent = pl.ds(0, sz.sent_rows)
    own = pltpu.make_async_copy(pack_ref.at[sent], out_ref.at[zone, sent], own_sem)
    own.start()
    pl.semaphore_wait(barrier, len(targets))
    copies = []
    for order, target in enumerate(targets):
        copy = pltpu.make_async_remote_copy(
            src_ref=pack_ref.at[sent],
            dst_ref=out_ref.at[zone, sent],
            send_sem=send_sem.at[order],
            recv_sem=recv_sem.at[order],
            device_id=target,
            device_id_type=MESH,
        )
        copy.start()
        copies.append(copy)
    own.wait()
    for copy in copies:
        copy.wait()


def resolve_zone(sz, zone, cat_ref, stage_ref, col_ref):
    shape = (HALF, LANES)
    member = cat_ref[zone, sz.member_row : sz.member_row + HALF, :].astype(jnp.int32)
    if isinstance(zone, int):
        before, after = max(zone - 1, 0), min(zone + 1, sz.zones - 1)
    else:
        before, after = jnp.maximum(zone - 1, 0), jnp.minimum(zone + 1, sz.zones - 1)
    low = member < sz.edge
    high = member >= sz.edge + sz.sources
    own = jnp.clip(member - sz.edge, 0, sz.sources - 1)
    rim = jnp.where(
        low, sz.edge + jnp.maximum(member, 0), jnp.where(high, member - sz.edge - sz.sources, 0)
    )
    lane = iota(shape, 1)
    for coord in range(2):
        rows = [
            cat_ref[zone, coord * sz.parts + part : coord * sz.parts + part + 1, :]
            for part in range(sz.parts)
        ]
        at = sz.edge_row + coord
        table = jnp.where(
            lane >= sz.edge,
            spread_rows(cat_ref[before, at : at + 1, :], shape),
            spread_rows(cat_ref[after, at : at + 1, :], shape),
        )
        place = jnp.where(low | high, take(table, rim), lookup(rows, own))
        if coord == 0:
            place = jnp.where(member < 0, FAR, place)
            start = zone * HALF if isinstance(zone, int) else pl.multiple_of(zone * HALF, HALF)
            stage_ref[pl.ds(start, HALF), :] = place
        else:
            col_ref[zone] = place


def spread_zone(sz, zone, turned_ref, row_ref):
    shape = (8, LANES)
    lane = iota(shape, 1)
    per = LANES // HALF
    index = (zone % per) * HALF + lane % HALF
    upper = lane % SLOTS >= HALF
    for part in range(sz.blobs // 8):
        pieces = []
        for half in range(2):
            at = half * sz.blobs + part * 8
            pieces.append(take(turned_ref[zone // per, at : at + 8, :], index))
        start = zone * sz.blobs + part * 8
        if not isinstance(zone, int):
            start = pl.multiple_of(start, 8)
        row_ref[pl.ds(start, 8), :] = jnp.where(upper, pieces[1], pieces[0])


def prepare(sz, cat_ref, shift_ref, amp_ref, sigma_ref, stage_ref, turned_ref, col_ref, row_ref, param_ref):
    each = (lambda body: [body(z) for z in range(sz.zones)]) if sz.zones <= 8 else (
        lambda body: lax.fori_loop(0, sz.zones, lambda z, c: (body(z), c)[1], 0)
    )
    sigma = sigma_ref[...]
    params = jnp.concatenate(
        [(-0.5 * LOG2E) / (sigma * sigma), amp_ref[...], shift_ref[...]], axis=0
    )
    param_ref[:, : params.shape[0]] = params.T
    each(lambda z: resolve_zone(sz, z, cat_ref, stage_ref, col_ref))
    for part in range(turned_ref.shape[0]):
        turned_ref[part] = stage_ref[part * LANES : (part + 1) * LANES, :].T
    each(lambda z: spread_zone(sz, z, turned_ref, row_ref))


def split(value):
    head = value.astype(jnp.bfloat16)
    return head, (value - head.astype(jnp.float32)).astype(jnp.bfloat16)


def tile_kernel(
    sz, blob_ref, band_ref, shift_ref, amp_ref, sigma_ref, cat_ref, pixel_ref, weight_ref,
    out_ref, stage_ref, turned_ref, col_ref, row_ref, param_ref, line_ref, rest_ref, used_ref,
):
    step = pl.program_id(0)
    per, height, _ = pixel_ref.shape

    @pl.when(step == 0)
    def _():
        out_ref[...] = jnp.zeros_like(out_ref)
        rest_ref[...] = jnp.zeros_like(rest_ref)
        for zone in range(sz.zones):
            used_ref[zone] = 0
        prepare(
            sz, cat_ref, shift_ref, amp_ref, sigma_ref,
            stage_ref, turned_ref, col_ref, row_ref, param_ref,
        )

    eight = (HALF, LANES)
    shape = (SLOTS, LANES)
    lane = iota(eight, 1)
    sub = iota(eight, 0)
    sub_f = sub.astype(jnp.float32)
    lane_f = lane.astype(jnp.float32)
    slots_all = COMPS * SLOTS
    width = COMPS * HALF
    keep = (iota(shape, 1) % HALF == iota(shape, 0) % HALF) & (iota(shape, 1) < 3 * width)
    keep = jnp.where(keep, 1.0, 0.0).astype(jnp.bfloat16)
    comp = lane // SLOTS % COMPS
    high_part = (lane < width) | (lane >= 2 * width)
    half_index = lane // HALF % COMPS * SLOTS + lane % HALF
    seat_a = lane // HALF == sub
    seat_b = lane // HALF == sub + HALF
    index_a = (sub + lane % HALF) % SLOTS
    index_b = (sub + HALF + lane % HALF) % SLOTS
    blank = jnp.zeros((LANES - 3 * width, LANES), jnp.float32)
    zero_tail = jnp.zeros((slots_all, LANES), jnp.bfloat16)
    zero_rows = jnp.zeros((LANES - 2 * slots_all, 2 * LANES), jnp.bfloat16)

    for slot in range(per):
        tile = step * per + slot
        blob = blob_ref[tile]
        zone = lax.div(blob, sz.blobs)
        local = lax.rem(blob, sz.blobs)
        param = spread_rows(param_ref[pl.ds(tile, 1), :], eight)
        pick = lambda k: take(param, jnp.full(eight, k, jnp.int32))
        row_rate = take(param, comp)
        row_amp = take(param, comp + COMPS)
        row_base = pick(2 * COMPS) + spread_rows(row_ref[pl.ds(blob, 1), :], eight)
        col_base = pick(2 * COMPS + 1)
        rate = [pick(g) for g in range(COMPS)]
        col_table = col_ref[zone]
        square = []
        for half in range(2):
            place = take(col_table, jnp.full(eight, half * sz.blobs, jnp.int32) + local)
            away = lane_f - col_base - place
            square.append(away * away)
        cols = [[jnp.exp2(rate[g] * square[half]) for half in range(2)] for g in range(COMPS)]
        heads, tails, heads_f, tails_f = [], [], [], []
        for g in range(COMPS):
            both = jnp.concatenate(cols[g], axis=0)
            head = both.astype(jnp.bfloat16)
            head_f = head.astype(jnp.float32)
            heads.append(head)
            heads_f.append(head_f)
            tails_f.append(both - head_f)
            tails.append(tails_f[-1].astype(jnp.bfloat16))
        rights = []
        for half in range(2):
            span = slice(half * HALF, (half + 1) * HALF)
            top = [h[span] for h in heads_f]
            rights.append(
                jnp.concatenate(top + top + [t[span] for t in tails_f] + [blank], axis=0).astype(
                    jnp.bfloat16
                )
            )
        rows = []
        for part in range(height // 8):
            away = (sub_f + 8.0 * part) - row_base
            value = jnp.exp2(row_rate * (away * away)) * row_amp
            rows.append(value)
            line_ref[slot, 0, part * 8 : (part + 1) * 8, :] = value
            for half in range(2):
                seen = take(value, half_index + half * HALF)
                head = seen.astype(jnp.bfloat16).astype(jnp.float32)
                line_ref[slot, 1 + half, part * 8 : (part + 1) * 8, :] = jnp.where(
                    high_part, head, seen - head
                )
        models = []
        for half in range(2):
            left = []
            for i in range(0, height, 2):
                pair = jnp.concatenate(
                    [
                        spread_rows(line_ref[slot, 1 + half, i + d : i + d + 1, :], eight)
                        for d in range(2)
                    ],
                    axis=0,
                )
                left.append(pair.astype(jnp.bfloat16) * keep)
            models.append(
                lax.dot_general(
                    jnp.concatenate(left, axis=0), rights[half], (((1,), (0,)), ((), ())),
                    preferred_element_type=jnp.float32,
                )
            )
        left = []
        for i in range(height):
            span = slice(i * HALF, (i + 1) * HALF)
            weight = spread_rows(weight_ref[slot, i : i + 1, :], shape)
            scaled = jnp.concatenate([models[0][span], models[1][span]], axis=0) * weight
            left.append(jnp.concatenate(split(scaled), axis=1))
        left.append(jnp.concatenate(split(weight_ref[slot] * pixel_ref[slot]), axis=1))
        top = jnp.concatenate(heads, axis=0)
        right = jnp.concatenate(
            [
                jnp.concatenate([top, top], axis=1),
                jnp.concatenate([jnp.concatenate(tails, axis=0), zero_tail], axis=1),
                zero_rows,
            ],
            axis=0,
        )
        product = lax.dot_general(
            jnp.concatenate(left, axis=0), right, (((1,), (1,)), ((), ())),
            preferred_element_type=jnp.float32,
        )
        normal = None
        for i in range(height):
            line = spread_rows(line_ref[slot, 0, i : i + 1, :], shape)
            term = product[i * SLOTS : (i + 1) * SLOTS] * line
            normal = term if normal is None else normal + term
        vector = None
        for part in range(height // 8):
            at = height * SLOTS + part * 8
            term = product[at : at + 8] * rows[part]
            vector = term if vector is None else vector + term
        folded = jnp.concatenate([normal, vector], axis=0)
        folded = folded + pltpu.roll(folded, LANES - slots_all, 1)
        folded = (
            folded
            + pltpu.roll(folded, LANES - SLOTS, 1)
            + pltpu.roll(folded, LANES - 2 * SLOTS, 1)
        )
        upper, lower, vector = folded[:HALF], folded[HALF:SLOTS], folded[SLOTS:]
        main = jnp.where(
            seat_a, take(upper, index_a), jnp.where(seat_b, take(lower, index_b), 0.0)
        )
        code = (
            lax.div(local, sz.share) * sz.systems
            + band_ref[tile] * sz.share
            + lax.rem(local, sz.share)
        )
        rest = jnp.where(lane == sub, take(upper, sub + HALF), 0.0)
        rest = jnp.where((lane >= SLOTS) & (lane < 2 * SLOTS), pltpu.roll(vector, SLOTS, 1), rest)
        rest = jnp.where((lane == HALF) & (sub == 0), code.astype(jnp.float32), rest)
        order = used_ref[zone]
        used_ref[zone] = order + 1
        out_ref[zone, pl.ds(order, 1), :] = jnp.sum(main, axis=0, keepdims=True)
        rest_ref[zone, pl.ds(order, 1), :] = jnp.sum(rest, axis=0, keepdims=True)

    @pl.when(step == pl.num_programs(0) - 1)
    def _():
        def body(zone, carry):
            total = rest_ref[zone, 0 : sz.rest, :]
            for seat in range(1, SEATS):
                piece = rest_ref[zone, seat * sz.rest : (seat + 1) * sz.rest, :]
                total = total + pltpu.roll(piece, seat * SEAT, 1)
            out_ref[zone, sz.capacity : sz.capacity + sz.rest, :] = total
            return carry

        lax.fori_loop(0, sz.zones, body, 0)


def tile_terms(sz, blob, band, shift, amp, sigma, catalogs, pixels, weights):
    tiles, height, width = pixels.shape
    per = TILES_STEP
    while tiles % per:
        per -= 1
    block = pl.BlockSpec((per, height, width), lambda s: (s, 0, 0))
    turned = -(-sz.zones * HALF // LANES)
    return pl.pallas_call(
        functools.partial(tile_kernel, sz),
        grid=(tiles // per,),
        out_shape=jax.ShapeDtypeStruct((sz.zones, sz.rows, LANES), jnp.float32),
        in_specs=[SMEM] * 2 + [VMEM] * 4 + [block, block],
        out_specs=pl.BlockSpec((sz.zones, sz.rows, LANES), lambda s: (0, 0, 0)),
        scratch_shapes=[
            pltpu.VMEM((turned * LANES, LANES), jnp.float32),
            pltpu.VMEM((turned, LANES, LANES), jnp.float32),
            pltpu.VMEM((sz.zones, HALF, LANES), jnp.float32),
            pltpu.VMEM((sz.zones * sz.blobs, LANES), jnp.float32),
            pltpu.VMEM((tiles, LANES), jnp.float32),
            pltpu.VMEM((per, 3, height, width), jnp.float32),
            pltpu.VMEM((sz.zones, sz.capacity, LANES), jnp.float32),
            pltpu.SMEM((sz.zones,), jnp.int32),
        ],
        compiler_params=pltpu.CompilerParams(dimension_semantics=("arbitrary",)),
    )(blob, band, shift, amp, sigma, catalogs, pixels, weights)


def find_seats(sz, zone, cat_ref, edge_ref, seat_ref):
    shape = (HALF, LANES)
    edges = spread_rows(edge_ref[...], shape)
    source = iota((sz.sources, LANES), 0)
    lane = iota((1, LANES), 1)
    total = None
    for side in range(3):
        near = lax.rem(zone + side - 1 + sz.zones, sz.zones)
        member = cat_ref[near, sz.member_row : sz.member_row + HALF, :].astype(jnp.int32)
        top = sz.edge + sz.sources
        if side == 0:
            valid = (member >= top) & (zone > 0)
            target = take(edges, jnp.where(valid, member - top, 0))
        elif side == 1:
            valid = (member >= sz.edge) & (member < top)
            target = member - sz.edge
        else:
            valid = (member >= 0) & (member < sz.edge) & (zone < sz.zones - 1)
            target = take(edges, jnp.where(valid, member + sz.edge, 0))
        target = jnp.where(valid, target, -1)
        for row in range(HALF):
            hit = source == target[row : row + 1, :]
            right = jnp.where(hit, 1.0, 0.0).astype(jnp.bfloat16)
            slot = side * SLOTS + row + lane // sz.blobs * HALF
            left = jnp.concatenate(
                [slot, lane % sz.blobs, jnp.zeros((SLOTS - 2, LANES), jnp.int32)], axis=0
            )
            part = lax.dot_general(
                left.astype(jnp.float32).astype(jnp.bfloat16), right, (((1,), (1,)), ((), ())),
                preferred_element_type=jnp.float32,
            )
            total = part if total is None else total + part
    seat_ref[...] = total[:8].astype(jnp.int32)


def gather_terms(sz, got_ref, table_ref, part_ref):
    for zone in range(sz.zones):
        start = zone * sz.capacity
        table_ref[start : start + sz.capacity, :LANES] = got_ref[zone, : sz.capacity, :]
        rest = got_ref[zone, sz.capacity : sz.capacity + sz.rest, :]
        for seat in range(SEATS):
            at = start + seat * sz.rest
            table_ref[at : at + sz.rest, LANES:] = (
                pltpu.roll(rest, LANES - seat * SEAT, 1) if seat else rest
            )
    square = (LANES, LANES)
    diagonal = iota(square, 0) == iota(square, 1)
    codes = []
    for at in range(0, sz.entries, LANES):
        block = table_ref[at : at + LANES, LANES:]
        code = take(block, jnp.full(square, HALF, jnp.int32))
        codes.append(jnp.sum(jnp.where(diagonal, code, 0.0), axis=0, keepdims=True))
    codes = jnp.concatenate(codes, axis=1)
    count = sz.bands * sz.block
    system = iota((count, sz.entries), 0)
    hit = jnp.where(system.astype(jnp.float32) == codes, 1.0, 0.0).astype(jnp.bfloat16)
    head, tail = split(table_ref[...])
    dims = (((1,), (0,)), ((), ()))
    total = lax.dot_general(hit, head, dims, preferred_element_type=jnp.float32)
    total = total + lax.dot_general(hit, tail, dims, preferred_element_type=jnp.float32)
    lane = iota((sz.third, LANES), 1) // SEAT
    for owner in range(sz.bands):
        start = owner * sz.block
        part_ref[owner, : sz.block, :] = total[start : start + sz.block, :LANES]
        rest = None
        for seat in range(FILTER_BANDS):
            at = start + seat * sz.third
            piece = total[at : at + sz.third, LANES:]
            piece = jnp.where(lane == seat, pltpu.roll(piece, seat * SEAT, 1) if seat else piece, 0.0)
            rest = piece if rest is None else rest + piece
        part_ref[owner, sz.block :, :] = rest


def solve(sz, summed, flat_ref, square_ref):
    main, rest = summed[: sz.block], summed[sz.block :]
    rest = jnp.concatenate(
        [pltpu.roll(rest, LANES - s * SEAT, 1) if s else rest for s in range(FILTER_BANDS)], axis=0
    )
    fill = jnp.zeros((LANES - sz.block, LANES), jnp.float32)
    flat_ref[:LANES, :] = jnp.concatenate([main, fill], axis=0).T
    flat_ref[LANES:, :] = jnp.concatenate([rest, fill], axis=0).T[: 2 * SLOTS]
    for l in range(SLOTS):
        for j in range(SLOTS):
            away = (l - j) % SLOTS
            if away < HALF:
                at = HALF * j + away
            elif away == HALF:
                at = LANES + min(j, l)
            else:
                at = HALF * l + SLOTS - away
            square_ref[l, j : j + 1, :] = flat_ref[at : at + 1, :]
    shape = (SLOTS, LANES)
    sub = iota(shape, 0)
    columns = [square_ref[l] + jnp.where(sub == l, PRIOR, 0.0) for l in range(SLOTS)]
    columns.append(flat_ref[LANES + SLOTS : LANES + 2 * SLOTS, :])
    scale = columns[0]
    for k in range(SLOTS):
        column = columns[k]
        inverse = 1.0 / column[k : k + 1]
        scale = jnp.where(sub == k, column, scale)
        column = jnp.where(sub == k, 0.0, column)
        for l in range(k + 1, SLOTS + 1):
            ratio = columns[l][k : k + 1] * inverse
            columns[l] = columns[l] - column * ratio
    return columns[SLOTS] / scale


def finish_kernel(
    sz, terms_ref, cat_ref, edge_ref, out_ref,
    got_ref, table_ref, part_ref, sum_ref, flat_ref, square_ref, solved_ref, flux_ref, seat_ref,
    send_term, recv_term, own_term, send_sum, recv_sum, send_flux, recv_flux,
):
    zones, bands = sz.zones, sz.bands
    zone = lax.axis_index("zone")
    band = lax.axis_index("band")
    at = lambda dz, db: (lax.rem(zone + dz, zones), lax.rem(band + db, bands))
    far = [(dz, 0) for dz in range(1, zones)]
    near = [(0, db) for db in range(1, bands)]
    sides = near + [(dz, db) for dz in (1, zones - 1) for db in range(bands)]
    greeted = far + [move for move in sides if move not in far]
    barrier = pltpu.get_barrier_semaphore()
    for move in greeted:
        pl.semaphore_signal(barrier, inc=1, device_id=at(*move), device_id_type=MESH)
    own = pltpu.make_async_copy(terms_ref.at[zone], got_ref.at[zone], own_term)
    own.start()
    pl.semaphore_wait(barrier, len(greeted))
    copies = []
    for order, move in enumerate(far):
        target = at(*move)
        copy = pltpu.make_async_remote_copy(
            src_ref=terms_ref.at[target[0]],
            dst_ref=got_ref.at[zone],
            send_sem=send_term.at[order],
            recv_sem=recv_term.at[order],
            device_id=target,
            device_id_type=MESH,
        )
        copy.start()
        copies.append(copy)
    find_seats(sz, zone, cat_ref, edge_ref, seat_ref)
    own.wait()
    for copy in copies:
        copy.wait()

    gather_terms(sz, got_ref, table_ref, part_ref)
    copies = []
    for order, move in enumerate(near):
        target = at(*move)
        copy = pltpu.make_async_remote_copy(
            src_ref=part_ref.at[target[1]],
            dst_ref=sum_ref.at[order],
            send_sem=send_sum.at[order],
            recv_sem=recv_sum.at[order],
            device_id=target,
            device_id_type=MESH,
        )
        copy.start()
        copies.append(copy)
    for copy in copies:
        copy.wait()
    summed = part_ref[band]
    for order in range(len(near)):
        summed = summed + sum_ref[order]
    solved = solve(sz, summed, flat_ref, square_ref)
    eight = (HALF, LANES)
    packed = jnp.where(
        iota(eight, 1) < LANES // 2, solved[:HALF], pltpu.roll(solved[HALF:], LANES // 2, 1)
    )
    solved_ref[...] = packed
    flux_ref[bands + band] = packed
    copies = []
    for order, move in enumerate(sides):
        side = {0: 1, 1: 0, zones - 1: 2}[move[0]]
        copy = pltpu.make_async_remote_copy(
            src_ref=solved_ref,
            dst_ref=flux_ref.at[side * bands + band],
            send_sem=send_flux.at[order],
            recv_sem=recv_flux.at[order],
            device_id=at(*move),
            device_id_type=MESH,
        )
        copy.start()
        copies.append(copy)
    for copy in copies:
        copy.wait()

    sub = iota(eight, 0)
    for part in range(sz.parts):
        span = slice(part * LANES, (part + 1) * LANES)
        slot = spread_rows(seat_ref[0:1, span], eight)
        blob = spread_rows(seat_ref[1:2, span], eight)
        row = slot % SLOTS
        key = slot // SLOTS * bands + blob // sz.share
        index = row // HALF * (LANES // 2) + blob % sz.share
        key = jnp.where(sub == row % HALF, key, -1)
        values = [jnp.zeros(eight, jnp.float32) for _ in range(FILTER_BANDS)]
        for table in range(3 * bands):
            flux = flux_ref[table]
            hit = key == table
            for k in range(FILTER_BANDS):
                values[k] = jnp.where(hit, take(flux, index + k * sz.share), values[k])
        out_ref[:, span] = jnp.concatenate(
            [jnp.sum(value, axis=0, keepdims=True) for value in values], axis=0
        )


def on_device(
    sizes, pixels, inv_var, tile_offset, psf_amp, psf_sigma, tile_blob, tile_band,
    source_pos, edge_rows, blob_members, sources_per_blob,
):
    zones, bands = sizes
    sz = Sizes(
        zones, bands, source_pos.shape[1], edge_rows.shape[0] // 2,
        sources_per_blob.shape[0], pixels.shape[0],
    )
    edges = edge_rows.reshape(1, -1)
    dma = pltpu.SemaphoreType.DMA
    catalogs = pl.pallas_call(
        functools.partial(catalog_kernel, sz),
        out_shape=jax.ShapeDtypeStruct((zones, sz.cat_rows, LANES), jnp.float32),
        in_specs=[VMEM] * 4,
        out_specs=VMEM,
        scratch_shapes=[
            pltpu.VMEM((sz.cat_rows, LANES), jnp.float32),
            dma((zones - 1,)), dma((zones - 1,)), dma,
        ],
        compiler_params=pltpu.CompilerParams(collective_id=0, has_side_effects=True),
    )(source_pos, edges, blob_members.T, sources_per_blob.reshape(1, -1))
    terms = tile_terms(
        sz, tile_blob, tile_band, tile_offset, psf_amp, psf_sigma, catalogs, pixels, inv_var
    )
    near = 3 * bands - 1
    rows = sz.block + sz.third
    return pl.pallas_call(
        functools.partial(finish_kernel, sz),
        out_shape=jax.ShapeDtypeStruct((FILTER_BANDS, sz.sources), jnp.float32),
        in_specs=[ANY, VMEM, VMEM],
        out_specs=VMEM,
        scratch_shapes=[
            pltpu.VMEM((zones, sz.rows, LANES), jnp.float32),
            pltpu.VMEM((sz.entries, 2 * LANES), jnp.float32),
            pltpu.VMEM((bands, rows, LANES), jnp.float32),
            pltpu.VMEM((bands - 1, rows, LANES), jnp.float32),
            pltpu.VMEM((LANES + 2 * SLOTS, LANES), jnp.float32),
            pltpu.VMEM((SLOTS, SLOTS, LANES), jnp.float32),
            pltpu.VMEM((HALF, LANES), jnp.float32),
            pltpu.VMEM((3 * bands, HALF, LANES), jnp.float32),
            pltpu.VMEM((8, sz.sources), jnp.int32),
            dma((zones - 1,)), dma((zones - 1,)), dma,
            dma((bands - 1,)), dma((bands - 1,)),
            dma((near,)), dma((near,)),
        ],
        compiler_params=pltpu.CompilerParams(collective_id=1, has_side_effects=True),
    )(terms, catalogs, edges)


def solution(mesh):
    sizes = (mesh.shape["zone"], mesh.shape["band"])
    return jax.shard_map(
        functools.partial(on_device, sizes),
        mesh=mesh,
        in_specs=(
            P(("zone", "band"), None, None),
            P(("zone", "band"), None, None),
            P(None, ("zone", "band")),
            P(None, ("zone", "band")),
            P(None, ("zone", "band")),
            P(("zone", "band")),
            P(("zone", "band")),
            P(None, "zone"),
            P("zone"),
            P("zone", None),
            P("zone"),
        ),
        out_specs=P(None, "zone"),
        check_vma=False,
    )
```

time: 83.4 us -> 63.2 us (0.76)
  Pallas kernels: 80.2 us -> 61.6 us
  local copies, waits for them, and re-layouts: 2.68 us -> 1.3 us
    pallas_call x6 -> x3, Pallas kernels: 80.2 us -> 61.6 us  [the longest x1 29.6 us: tile_terms(): pl.pallas_call(functools.partial(tile_kernel, sz), grid=(tiles // per,),...]
    unnamed x2 -> x1, local copies, waits for them, and re-layouts: 2.68 us -> 1.3 us
where the time goes in v1:
time: 63.2 us; the launch traced here: 63 us
  Pallas kernels  61.6 us (97%)
  local copies, waits for them, and re-layouts  1.3 us (2%)
    pallas_call x1, Pallas kernels, tile_terms(): pl.pallas_call(functools.partial(tile_kernel, sz), grid=(tiles // per,),...  29.6 us
    pallas_call x1, Pallas kernels, on_device(): pl.pallas_call(functools.partial(finish_kernel, sz), out_shape=jax.ShapeD...  21.9 us
    pallas_call x1, Pallas kernels, on_device(): pl.pallas_call(functools.partial(catalog_kernel, sz), out_shape=jax.Shape...  10.1 us
    unnamed x1, local copies, waits for them, and re-layouts  1.3 us

profile of v1, /device:TPU:0, one launch (start us, length us, event | category | flops | bytes accessed | tf_op | source)
XLA Modules:
  0.0 63.0 jit_solution(8331682479461853318)
XLA Ops:
  0.0 10.1 %shard_map.109.cat_ref = f32[8,24,128]{2,1,0:T(8,128)} custom-call(f32[2,512]{1,0:T(2,128)} %source_ref.1, s32[1,128]{1,0:T(1,128)} %bitcast.4, s32[16,64]{1,0:T(8,128)} %bitcast.3, s32[1,64]{1,0:T(1,128)} %bitcast.6), custom_call_target="tpu_custom_call" | custom-call | tf_op jit(solution)/shard_map/pallas_call | solution.py:604
  10.1 29.6 %shard_map.110.terms_ref = f32[8,40,128]{2,1,0:T(8,128)} custom-call(s32[128]{0:T(128)} %blob_ref.1, s32[128]{0:T(128)} %band_ref.1, f32[2,128]{1,0:T(2,128)} %shift_ref.1, f32[3,128]{1,0:T(4,128)} %amp_ref.1, f32[3,128]{1,0:T(4,128)} %sigma_ref.1, f32[8,24,128]{2,1,0:T(8,128)} %shard_map.109.cat_ref, f32[128,32,128]{2,1,0:T(8,128)} %pixel_ref.1, ...), custom_call_target="tpu_custom_call" | custom-call | tf_op jit(solution)/shard_map/pallas_call | solution.py:367
  39.8 21.9 %shard_map.111 = f32[3,512]{1,0:T(4,128)} custom-call(f32[8,40,128]{2,1,0:T(8,128)} %shard_map.110.terms_ref, f32[8,24,128]{2,1,0:T(8,128)} %shard_map.109.cat_ref, s32[1,128]{1,0:T(1,128)} %bitcast.5), custom_call_target="tpu_custom_call" | custom-call | tf_op jit(solution)/shard_map/pallas_call | solution.py:620
  61.7 1.3 %copy.13 = f32[3,512]{1,0:T(4,128)} copy(f32[3,512]{1,0:T(4,128)} %shard_map.111) | data formatting | bytes 12288
